TPU v7x, 32 devices: a whole 2x2x4 slice. The times are simulated.
32 devices in a mesh: gy: 8 (over y, x, core), gz: 4 (over z).
Axes of the slice: x: 2, y: 2, z: 4, core: 2. Of those that a mesh axis runs over, the one named last changes fastest.
Arguments:
- initial_warmth: float32 [1024, 32, 512], P('gy', None, 'gz'), may hold values from -18 to 18
- transverse_factor: float32 [32, 512], P(None, 'gz'), may hold values from 0.05 to 0.24
- energy_supply_series: float32 [1024, 32, 512], P('gy', None, 'gz'), may hold values from -1.5 to 1.5
Outputs:
- temperature_next: float32 [1024, 32, 512], P('gy', None, 'gz')
All inputs are finite; a program needn't handle non-finite values.
Results may differ from a plain program's by a relative error of at most 0.0001.
Values sent between devices are 32-bit elements; how exact they have to be, the bound alone decides.
A program may use at most 64 MiB of HBM per device.

v0:
```python
import jax
import jax.numpy as jnp
import numpy as np
from jax import lax
from jax.sharding import PartitionSpec as P

coupling = 400.0


def tables(m, parts):
    root = (1.0 + 2.0 * coupling - np.sqrt(1.0 + 4.0 * coupling)) / (2.0 * coupling)
    height = 1.0 / (1.0 + 2.0 * coupling - 2.0 * coupling * root)
    delta = (1.0 + root**2) / (1.0 - root**2)
    cell = np.arange(m)
    distance = np.abs(cell[:, None] - cell[None, :])
    local = np.concatenate(
        [height**2 * (delta + distance) * root**distance, height * root**distance], axis=1
    )
    rows = []
    for reach in (m - 1 - cell, cell):
        fall = root**reach
        rows.append(np.concatenate([height**2 * fall, 0.0 * fall]))
        rows.append(np.concatenate([height**2 * (delta + reach) * fall, height * fall]))
    sums = np.stack(rows)
    step = root**m
    whole = step**parts
    mix = np.zeros((parts, 4, parts, 4))
    for d in range(parts):
        for p in range(1, parts + 1):
            near = step ** (p - 1) / (1.0 - whole)
            far = (
                m * step ** (p - 1) * ((p - 1) / (1.0 - whole) + parts * whole / (1.0 - whole) ** 2)
            )
            for first, other in ((0, (d - p) % parts), (2, (d + p) % parts)):
                mix[d, first, other, first] = near
                mix[d, first + 1, other, first + 1] = near
                mix[d, first + 1, other, first] = far
    columns = []
    for reach in (cell + 1, m - cell):
        columns += [reach * root**reach, root**reach]
    spread = np.stack(columns, axis=1)
    return [t.astype(np.float32) for t in (local, sums, mix, spread)]


def shifted(block, axis, by):
    count = lax.axis_size(axis)
    return lax.ppermute(block, axis, [(i, (i + by) % count) for i in range(count)])


def transverse(wide, c):
    mid = wide[..., 1:-1]
    around = jnp.roll(mid, 1, -2) + jnp.roll(mid, -1, -2) + wide[..., 2:] + wide[..., :-2]
    return mid + c * (around - 4.0 * mid)


def per_device(field, c, q):
    m, ny, nz = field.shape
    parts = lax.axis_size("gy")
    local, sums, mix, spread = tables(m, parts)

    def edges(a, b, at):
        planes = [field[:, :, a], field[:, :, b], q[:, :, at]]
        return jnp.concatenate(planes + [c[None, :, at]], axis=0)

    low = shifted(edges(nz - 2, nz - 1, nz - 1), "gz", 1)
    high = shifted(edges(1, 0, 0), "gz", -1)

    def plane(packed, k):
        return packed[k * m : (k + 1) * m, :, None]

    wide_field = jnp.concatenate(
        [plane(low, 0), plane(low, 1), field, plane(high, 1), plane(high, 0)], axis=2
    )
    wide_q = jnp.concatenate([plane(low, 2), q, plane(high, 2)], axis=2)
    wide_c = jnp.concatenate([low[3 * m, :, None], c, high[3 * m, :, None]], axis=1)
    g = transverse(transverse(wide_field, wide_c), c)
    h = transverse(wide_q, c)
    both = jnp.concatenate([g, h], axis=0)

    def dot(a, b):
        return lax.dot_general(
            a,
            b,
            (((1,), (0,)), ((), ())),
            precision=lax.Precision.HIGH,
            preferred_element_type=jnp.float32,
        )

    planes = dot(jnp.asarray(sums), both)
    gathered = lax.all_gather(planes, "gy", axis=0, tiled=True)
    mine = lax.dynamic_index_in_dim(
        jnp.asarray(mix.reshape(parts, 4, parts * 4)), lax.axis_index("gy"), 0, False
    )
    incoming = dot(mine, gathered)
    return dot(jnp.asarray(local), both) + dot(jnp.asarray(spread), incoming) + q


def solution(mesh):
    placed = (P("gy", None, "gz"), P(None, "gz"), P("gy", None, "gz"))
    return jax.shard_map(
        per_device, mesh=mesh, in_specs=placed, out_specs=P("gy", None, "gz"), check_vma=False
    )
```

profile of v0, /device:TPU:0, one launch (start us, length us, event | category | flops | bytes accessed | tf_op | source)
XLA Modules:
  0.0 71.5 jit_solution(9735770621171226381)
XLA Ops:
  0.0 8.7 %fusion.28 = (f32[128,32,1]{2,1,0:T(8,128)}, f32[128,32,1]{2,1,0:T(8,128)}, f32[128,32,1]{2,1,0:T(8,128)}, f32[128,32,1]{2,1,0:T(8,128)}) fusion(f32[128,32,128]{2,1,0:T(8,128)} %param.7), kind=kLoop, calls=%fused_computation.45 | loop fusion | bytes 131072 | tf_op jit(solution)/shard_map/slice | solution.py:62
  8.7 0.0 copy-start.2
  8.7 2.8 %copy.96 = f32[128,32,1]{0,1,2:T(8,128)S(1)} copy(f32[128,32,1]{2,1,0:T(8,128)} %get-tuple-element.19) | data formatting | bytes 32768
  11.5 2.7 %copy.97 = f32[128,32,1]{0,1,2:T(8,128)S(1)} copy(f32[128,32,1]{2,1,0:T(8,128)} %get-tuple-element.18) | data formatting | bytes 32768
  14.2 0.0 copy-done.2
  14.2 2.8 %fusion.29 = (f32[128,32,1]{2,1,0:T(8,128)}, f32[128,32,1]{2,1,0:T(8,128)}) fusion(f32[128,32,128]{2,1,0:T(8,128)S(1)} %copy-done.2), kind=kLoop, calls=%fused_computation.46 | loop fusion | bytes 65536 | tf_op jit(solution)/shard_map/slice | solution.py:62
  16.9 0.0 copy-start.6
  16.9 2.7 %copy.98 = f32[128,32,1]{0,1,2:T(8,128)S(1)} copy(f32[128,32,1]{2,1,0:T(8,128)} %get-tuple-element.22) | data formatting | bytes 32768
  19.6 0.0 copy-done.6
  19.6 0.1 slice_bitcast_fusion.2
  19.7 3.1 %collective-permute-start = (f32[385,32]{0,1:T(8,128)S(1)}, f32[385,32]{0,1:T(8,128)S(1)}, u32[]{:S(2)}, u32[]{:S(2)}) collective-permute-start(f32[385,32]{0,1:T(8,128)S(1)} %pad_maximum_fusion.8), channel_id=1, source_target_pairs={{0,1},{1,2},{2,3},{3,0},{4,5},{5,6},{6,7},{7,4},{8,9},{9,10},{10,1... | collective-permute-start | bytes 147848 | tf_op jit(solution)/shard_map/ppermute | solution.py:47
  22.8 2.7 %copy.99 = f32[128,32,1]{0,1,2:T(8,128)S(1)} copy(f32[128,32,1]{2,1,0:T(8,128)} %get-tuple-element.17) | data formatting | bytes 32768
  25.4 2.7 %copy.100 = f32[128,32,1]{0,1,2:T(8,128)S(1)} copy(f32[128,32,1]{2,1,0:T(8,128)} %get-tuple-element.20) | data formatting | bytes 32768
  28.1 2.7 %copy.101 = f32[128,32,1]{0,1,2:T(8,128)S(1)} copy(f32[128,32,1]{2,1,0:T(8,128)} %get-tuple-element.21) | data formatting | bytes 32768
  30.7 2.3 %collective-permute-start.1 = (f32[385,32]{0,1:T(8,128)S(1)}, f32[385,32]{0,1:T(8,128)S(1)}, u32[]{:S(2)}, u32[]{:S(2)}) collective-permute-start(f32[385,32]{0,1:T(8,128)S(1)} %pad_maximum_fusion.9), channel_id=1, source_target_pairs={{0,3},{1,0},{2,1},{3,2},{4,7},{5,4},{6,5},{7,6},{8,11},{9,8},{10,9... | collective-permute-start | bytes 147848 | tf_op jit(solution)/shard_map/ppermute | solution.py:47
  33.0 1.9 %copy.89 = f32[128,32,128]{0,2,1:T(8,128)} copy(f32[128,32,128]{2,1,0:T(8,128)S(1)} %copy-done.2) | data formatting | bytes 4194304 | tf_op args[2]
  34.9 0.0 copy-start
  34.9 4.8 %fusion.26 = (f32[128,31,128]{0,2,1:T(8,128)}, f32[128,31,128]{0,2,1:T(8,128)}) fusion(f32[128,32,128]{0,2,1:T(8,128)} %copy.89), kind=kLoop, calls=%fused_computation.43 | loop fusion | bytes 8126464 | tf_op jit(solution)/shard_map/jit(_roll_static)/slice | solution.py:52
  39.7 0.9 %fusion.27 = (f32[128,1,128]{0,2,1:T(8,128)S(1)}, f32[128,1,128]{0,2,1:T(8,128)S(1)}) fusion(f32[128,32,128]{0,2,1:T(8,128)} %copy.89), kind=kLoop, calls=%fused_computation.44 | loop fusion | bytes 262144 | tf_op jit(solution)/shard_map/jit(_roll_static)/slice | solution.py:52
  40.6 0.0 copy-done
  40.6 1.9 %copy.72 = f32[128,32,128]{0,2,1:T(8,128)} copy(f32[128,32,128]{2,1,0:T(8,128)S(1)} %copy-done) | data formatting | bytes 4194304 | tf_op args[0]
  42.4 0.0 collective-permute-done
  42.4 0.0 collective-permute-done.1
  42.5 1.8 %pad_maximum_fusion.3 = f32[128,32,130]{0,2,1:T(8,128)S(1)} fusion(f32[128,32,1]{0,2,1:T(1,128)S(1)} %bitcast.44, f32[128,32,128]{0,2,1:T(8,128)} %copy.72, f32[128,32,1]{0,2,1:T(1,128)S(1)} %bitcast.42), kind=kLoop, calls=%fused_computation.3 | loop fusion | flops 1064960 | bytes 4259840 | tf_op jit(solution)/shard_map/concatenate | solution.py:71
  44.3 0.0 copy-start.3
  44.3 0.3 fusion.24
  44.6 0.1 pad_maximum_fusion.10
  44.7 1.2 %copy-done.3 = f32[128,32,128]{0,2,1:T(8,128)S(1)} copy-done((f32[128,32,128]{0,2,1:T(8,128)S(1)}, f32[128,32,128]{0,2,1:T(8,128)}, u32[]{:S(2)}) %copy-start.3) | copy-done | bytes 2097176
  45.8 1.5 %fusion.6 = f32[128,32,130]{0,2,1:T(8,128)S(1)} fusion(f32[128,31,130]{0,2,1:T(8,128)S(1)} %get-tuple-element.10, f32[128,1,130]{0,2,1:T(8,128)S(1)} %get-tuple-element.12, f32[128,1,130]{0,2,1:T(8,128)S(1)} %get-tuple-element.11, f32[128,31,130]{0,2,1:T(8,128)S(1)} %get-tuple-element.9, f32[128,32,1]{0,2,1:T(1,128)S(1)} %bitcast.47, ...), kind=kLoop, calls=%fused_computation.9 | loop fusion | flops 7987200 | bytes 8569088 | tf_op jit(solution)/shard_map/add | solution.py:53
  47.4 0.0 copy-start.1
  47.4 0.0 copy-start.4
  47.4 0.0 copy-start.5
  47.4 0.5 fusion.22
  47.9 1.0 %copy-done.1 = f32[128,32,128]{0,2,1:T(8,128)S(1)} copy-done((f32[128,32,128]{0,2,1:T(8,128)S(1)}, f32[128,32,128]{0,2,1:T(8,128)}, u32[]{:S(2)}) %copy-start.1) | copy-done | bytes 2097176
  49.0 0.6 copy-done.4
  49.6 0.6 copy-done.5
  50.2 0.0 copy-start.8
  50.2 2.4 %fusion.14 = (f32[128,32,128]{0,2,1:T(8,128)S(1)}, f32[128,32,128]{0,2,1:T(8,128)S(1)}) fusion(f32[128,32,130]{0,2,1:T(8,128)S(1)} %fusion.6, f32[128,31,128]{0,2,1:T(8,128)S(1)} %get-tuple-element.6, f32[128,1,128]{0,2,1:T(8,128)S(1)} %get-tuple-element.8, f32[128,1,128]{0,2,1:T(8,128)S(1)} %get-tuple-element.7, f32[128,31,128]{0,2,1:T(8,128)S(1)} %get-tuple-element.5, ...), kind=kLoop, calls=%fused_computation.20 | loop fusion | flops 10485760 | bytes 21020672 | tf_op jit(solution)/shard_map/add | solution.py:53
  52.6 0.0 copy-done.8
  52.6 0.0 copy-start.9
  52.6 1.8 %fusion = f32[4,32,128]{2,0,1:T(4,128)S(1)} fusion(f32[4,256,1]{1,0,2:T(4,128)S(1)} %copy-done.8, f32[128,32,128]{0,2,1:T(8,128)S(1)} %get-tuple-element.30, f32[128,32,128]{0,2,1:T(8,128)S(1)} %get-tuple-element.29), kind=kOutput, calls=%fused_computation.1 | convolution fusion | flops 26214400 | bytes 4263936 | tf_op jit(solution)/shard_map/dot_general | solution.py:81
  54.4 10.2 %all_gather.3 = f32[32,32,128]{2,1,0:T(8,128)S(1)} all-gather(f32[4,32,128]{2,1,0:T(8,128)S(1)} %copy.91), channel_id=1, replica_groups=mesh['gy'=8,'gz'=4] {'gy'}, dimensions={0}, use_global_device_ids=true | all-gather | bytes 589824 | tf_op jit(solution)/shard_map/all_gather | solution.py:90
  64.6 1.2 %fusion.15 = f32[4,32,128]{2,0,1:T(4,128)S(1)} fusion(f32[32,32,128]{2,1,0:T(8,128)S(1)} %all_gather.3, f32[8,4,32]{2,1,0:T(4,128)} %constant.24.clone, s32[]{:T(128)S(6)} %select_n.4), kind=kOutput, calls=%fused_computation.25 | convolution fusion | flops 3145728 | bytes 591876 | tf_op jit(solution)/shard_map/dot_general | solution.py:81
  65.8 0.0 copy-done.9
  65.8 1.8 %fusion.32 = f32[32,128,128]{2,1,0:T(8,128)S(1)} fusion(f32[4,32,128]{2,0,1:T(4,128)S(1)} %fusion.15, f32[128,4,1]{0,1,2:T(4,128)S(1)} %copy-done.9), kind=kOutput, calls=%fused_computation.49 | convolution fusion | flops 12582912 | bytes 2164736 | tf_op jit(solution)/shard_map/dot_general | solution.py:81
  67.7 0.0 copy-done.7
  67.7 1.9 %bitcast_add_fusion = f32[128,32,128]{0,2,1:T(8,128)S(1)} fusion(f32[128,32,128]{0,2,1:T(8,128)S(1)} %copy-done.1, f32[32,128,128]{2,1,0:T(8,128)S(1)} %fusion.32, f32[128,256,1]{1,0,2:T(8,128)S(1)} %copy-done.7, f32[128,32,128]{0,2,1:T(8,128)S(1)} %get-tuple-element.30, f32[128,32,128]{0,2,1:T(8,128)S(1)} %get-tuple-element.29), kind=kOutput, calls=%fused_computation.24 | convolution fusion | flops 807403520 | bytes 10616832 | tf_op jit(solution)/shard_map/dot_general | solution.py:81
  69.6 2.0 %copy.94 = f32[128,32,128]{2,1,0:T(8,128)} copy(f32[128,32,128]{0,2,1:T(8,128)S(1)} %bitcast_add_fusion) | data formatting | bytes 4194304 | tf_op jit(solution)/shard_map/add | solution.py:95
  (10 shorter events, 0.1 us)
Async XLA Ops:
  8.7 5.5 %copy-start.2 = (f32[128,32,128]{2,1,0:T(8,128)S(1)}, f32[128,32,128]{2,1,0:T(8,128)}, u32[]{:S(2)}) copy-start(f32[128,32,128]{2,1,0:T(8,128)} %param.9) | copy-start | bytes 6291460
  16.9 2.7 %copy-start.6 = (f32[32,128]{1,0:T(8,128)S(1)}, f32[32,128]{1,0:T(8,128)}, u32[]{:S(2)}) copy-start(f32[32,128]{1,0:T(8,128)} %param.8) | copy-start | bytes 49156
  19.7 22.8 %collective-permute-start = (f32[385,32]{0,1:T(8,128)S(1)}, f32[385,32]{0,1:T(8,128)S(1)}, u32[]{:S(2)}, u32[]{:S(2)}) collective-permute-start(f32[385,32]{0,1:T(8,128)S(1)} %pad_maximum_fusion.8), channel_id=1, source_target_pairs={{0,1},{1,2},{2,3},{3,0},{4,5},{5,6},{6,7},{7,4},{8,9},{9,10},{10,1... | collective-permute-start | bytes 147848 | tf_op jit(solution)/shard_map/ppermute | solution.py:47
  30.7 11.7 %collective-permute-start.1 = (f32[385,32]{0,1:T(8,128)S(1)}, f32[385,32]{0,1:T(8,128)S(1)}, u32[]{:S(2)}, u32[]{:S(2)}) collective-permute-start(f32[385,32]{0,1:T(8,128)S(1)} %pad_maximum_fusion.9), channel_id=1, source_target_pairs={{0,3},{1,0},{2,1},{3,2},{4,7},{5,4},{6,5},{7,6},{8,11},{9,8},{10,9... | collective-permute-start | bytes 147848 | tf_op jit(solution)/shard_map/ppermute | solution.py:47
  34.9 5.7 %copy-start = (f32[128,32,128]{2,1,0:T(8,128)S(1)}, f32[128,32,128]{2,1,0:T(8,128)}, u32[]{:S(2)}) copy-start(f32[128,32,128]{2,1,0:T(8,128)} %param.7) | copy-start | bytes 6291460
  44.3 1.6 %copy-start.3 = (f32[128,32,128]{0,2,1:T(8,128)S(1)}, f32[128,32,128]{0,2,1:T(8,128)}, u32[]{:S(2)}) copy-start(f32[128,32,128]{0,2,1:T(8,128)} %copy.72) | copy-start | bytes 6291460
  47.4 1.6 %copy-start.1 = (f32[128,32,128]{0,2,1:T(8,128)S(1)}, f32[128,32,128]{0,2,1:T(8,128)}, u32[]{:S(2)}) copy-start(f32[128,32,128]{0,2,1:T(8,128)} %copy.89) | copy-start | bytes 6291460
  47.4 2.2 %copy-start.4 = (f32[128,31,128]{0,2,1:T(8,128)S(1)}, f32[128,31,128]{0,2,1:T(8,128)}, u32[]{:S(2)}) copy-start(f32[128,31,128]{0,2,1:T(8,128)} %get-tuple-element.13) | copy-start | bytes 6094852
  47.4 2.8 %copy-start.5 = (f32[128,31,128]{0,2,1:T(8,128)S(1)}, f32[128,31,128]{0,2,1:T(8,128)}, u32[]{:S(2)}) copy-start(f32[128,31,128]{0,2,1:T(8,128)} %get-tuple-element.14) | copy-start | bytes 6094852
  50.2 2.4 %copy-start.8 = (f32[4,256,1]{1,0,2:T(4,128)S(1)}, f32[4,256,1]{1,0,2:T(4,128)}, u32[]{:S(2)}) copy-start(f32[4,256,1]{1,0,2:T(4,128)} %constant.28) | copy-start | bytes 12292
  52.6 13.2 %copy-start.9 = (f32[128,4,1]{0,1,2:T(4,128)S(1)}, f32[128,4,1]{0,1,2:T(4,128)}, u32[]{:S(2)}) copy-start(f32[128,4,1]{0,1,2:T(4,128)} %constant.29) | copy-start | bytes 6148
  54.4 13.2 %copy-start.7 = (f32[128,256,1]{1,0,2:T(8,128)S(1)}, f32[128,256,1]{1,0,2:T(8,128)}, u32[]{:S(2)}) copy-start(f32[128,256,1]{1,0,2:T(8,128)} %constant.27) | copy-start | bytes 393220
where the time goes:
time: 72 us; the launch traced here: 71.5 us
  local copies, waits for them, and re-layouts  43.3 us (60%)
  blocking collectives  10.2 us (14%)
  matrix products  6.71 us (9%)
  other arithmetic  5.76 us (8%)
  starting transfers between devices  5.36 us (7%)
    unnamed x28, local copies, waits for them, and re-layouts  23.3 us
    slice x2, local copies, waits for them, and re-layouts, edges(): planes = [field[:, :, a], field[:, :, b], q[:, :, at]]  11.5 us
    all_gather x1, blocking collectives, per_device(): gathered = lax.all_gather(planes, 'gy', axis=0, tiled=True)  10.2 us
    dot_general x4, matrix products, dot(): lax.dot_general(a, b, (((1,), (0,)), ((), ())), precision=lax.Precision.H...  6.71 us
    slice x6, local copies, waits for them, and re-layouts, transverse(): jnp.roll(mid, -1, -2)  6.49 us
    ppermute x2, starting transfers between devices, shifted(): lax.ppermute(block, axis, [(i, (i + by) % count) for i in range(count)])  5.36 us
    add x2, other arithmetic, transverse(): return mid + c * (around - 4.0 * mid)  3.89 us
    add x1, local copies, waits for them, and re-layouts, per_device(): dot(jnp.asarray(local), both) + dot(jnp.asarray(spread), incoming) + q  1.97 us
  transfers between devices with their start and end apart: 2, of which 0 were waited for; matrix products, arithmetic and copies ran while one was open for 24% of the time, Pallas kernels for 0%

commit v1 on v0

--- a/solution.py
+++ b/solution.py
@@ -87,7 +87,12 @@
         )
 
     planes = dot(jnp.asarray(sums), both)
-    gathered = lax.all_gather(planes, "gy", axis=0, tiled=True)
+    ring = [planes]
+    for hop in range(7):
+        ring.append(lax.ppermute(ring[-1], "gy", [(dev, (dev + 1) % 8) for dev in range(8)]))
+    gathered = jnp.roll(
+        jnp.concatenate(ring[::-1], axis=0), (lax.axis_index("gy") + 1) * ring[0].shape[0], axis=0
+    )
     mine = lax.dynamic_index_in_dim(
         jnp.asarray(mix.reshape(parts, 4, parts * 4)), lax.axis_index("gy"), 0, False
     )

time: 72 us -> 101 us (1.40)
  waiting for transfers between devices: 0.01 us -> 31.6 us
  blocking collectives: 10.2 us -> 0 us
  local copies, waits for them, and re-layouts: 43.3 us -> 47.4 us
  matrix products: 6.71 us -> 9.6 us
    ppermute x0 -> x7, waiting for transfers between devices: none -> 31.6 us  [per_device(): lax.ppermute(ring[-1], 'gy', [(dev, (dev + 1) % 8) for dev in range(8)])]
    all_gather x1 -> x0, blocking collectives: 10.2 us -> none  [per_device(): gathered = lax.all_gather(planes, 'gy', axis=0, tiled=True)]
    dot_general x4, matrix products: 6.71 us -> 9.6 us  [dot(): lax.dot_general(a, b, (((1,), (0,)), ((), ())), precision=lax.Precision.H...]
    concatenate x0 -> x1, local copies, waits for them, and re-layouts: none -> 2.26 us  [per_device(): jnp.roll(jnp.concatenate(ring[::-1], axis=0), (lax.axis_index('gy') + 1)...]
    add x1, local copies, waits for them, and re-layouts: 1.97 us -> 3.03 us  [per_device(): dot(jnp.asarray(local), both) + dot(jnp.asarray(spread), incoming) + q]
    unnamed x28 -> x36, local copies, waits for them, and re-layouts: 23.3 us -> 24.1 us
  transfers between devices with their start and end apart: 2 -> 9, of which waited for: 0 -> 7; matrix products, arithmetic and copies ran while one was open for 24% -> 17% of each run, Pallas kernels for 0% -> 0%
where the time goes in v1:
time: 101 us; the launch traced here: 100 us
  local copies, waits for them, and re-layouts  47.4 us (47%)
  waiting for transfers between devices  31.6 us (31%)
  matrix products  9.6 us (10%)
  other arithmetic  5.75 us (6%)
  starting transfers between devices  5.37 us (5%)
    ppermute x7, waiting for transfers between devices, per_device(): lax.ppermute(ring[-1], 'gy', [(dev, (dev + 1) % 8) for dev in range(8)])  31.6 us
    unnamed x36, local copies, waits for them, and re-layouts  24.1 us
    slice x2, local copies, waits for them, and re-layouts, edges(): planes = [field[:, :, a], field[:, :, b], q[:, :, at]]  11.5 us
    dot_general x4, matrix products, dot(): lax.dot_general(a, b, (((1,), (0,)), ((), ())), precision=lax.Precision.H...  9.6 us
    slice x6, local copies, waits for them, and re-layouts, transverse(): jnp.roll(mid, -1, -2)  6.49 us
    ppermute x2, starting transfers between devices, shifted(): lax.ppermute(block, axis, [(i, (i + by) % count) for i in range(count)])  5.36 us
    add x2, other arithmetic, transverse(): return mid + c * (around - 4.0 * mid)  3.89 us
    add x1, local copies, waits for them, and re-layouts, per_device(): dot(jnp.asarray(local), both) + dot(jnp.asarray(spread), incoming) + q  3.03 us
  transfers between devices with their start and end apart: 9, of which 7 were waited for; matrix products, arithmetic and copies ran while one was open for 17% of the time, Pallas kernels for 0%

profile of v1, /device:TPU:0, one launch (start us, length us, event | category | flops | bytes accessed | tf_op | source)
XLA Modules:
  0.0 100.0 jit_solution(4480089155977413728)
XLA Ops:
  0.0 8.7 %fusion.28 = (f32[128,32,1]{2,1,0:T(8,128)}, f32[128,32,1]{2,1,0:T(8,128)}, f32[128,32,1]{2,1,0:T(8,128)}, f32[128,32,1]{2,1,0:T(8,128)}) fusion(f32[128,32,128]{2,1,0:T(8,128)} %param.7), kind=kLoop, calls=%fused_computation.45 | loop fusion | bytes 131072 | tf_op jit(solution)/shard_map/slice | solution.py:62
  8.7 2.8 %copy.67 = f32[128,32,1]{0,1,2:T(8,128)S(1)} copy(f32[128,32,1]{2,1,0:T(8,128)} %get-tuple-element.19) | data formatting | bytes 32768
  11.6 2.7 %copy.68 = f32[128,32,1]{0,1,2:T(8,128)S(1)} copy(f32[128,32,1]{2,1,0:T(8,128)} %get-tuple-element.18) | data formatting | bytes 32768
  14.2 2.8 %fusion.29 = (f32[128,32,1]{2,1,0:T(8,128)}, f32[128,32,1]{2,1,0:T(8,128)}) fusion(f32[128,32,128]{2,1,0:T(8,128)S(1)} %copy-done.5), kind=kLoop, calls=%fused_computation.46 | loop fusion | bytes 65536 | tf_op jit(solution)/shard_map/slice | solution.py:62
  17.0 2.7 %copy.69 = f32[128,32,1]{0,1,2:T(8,128)S(1)} copy(f32[128,32,1]{2,1,0:T(8,128)} %get-tuple-element.22) | data formatting | bytes 32768
  19.6 0.1 slice_bitcast_fusion.2
  19.7 3.1 %collective-permute-start = (f32[385,32]{0,1:T(8,128)S(1)}, f32[385,32]{0,1:T(8,128)S(1)}, u32[]{:S(2)}, u32[]{:S(2)}) collective-permute-start(f32[385,32]{0,1:T(8,128)S(1)} %pad_maximum_fusion.8), channel_id=1, source_target_pairs={{0,1},{1,2},{2,3},{3,0},{4,5},{5,6},{6,7},{7,4},{8,9},{9,10},{10,1... | collective-permute-start | bytes 147848 | tf_op jit(solution)/shard_map/ppermute | solution.py:47
  22.8 2.7 %copy.70 = f32[128,32,1]{0,1,2:T(8,128)S(1)} copy(f32[128,32,1]{2,1,0:T(8,128)} %get-tuple-element.17) | data formatting | bytes 32768
  25.5 2.7 %copy.71 = f32[128,32,1]{0,1,2:T(8,128)S(1)} copy(f32[128,32,1]{2,1,0:T(8,128)} %get-tuple-element.20) | data formatting | bytes 32768
  28.1 2.7 %copy.72 = f32[128,32,1]{0,1,2:T(8,128)S(1)} copy(f32[128,32,1]{2,1,0:T(8,128)} %get-tuple-element.21) | data formatting | bytes 32768
  30.8 2.3 %collective-permute-start.1 = (f32[385,32]{0,1:T(8,128)S(1)}, f32[385,32]{0,1:T(8,128)S(1)}, u32[]{:S(2)}, u32[]{:S(2)}) collective-permute-start(f32[385,32]{0,1:T(8,128)S(1)} %pad_maximum_fusion.9), channel_id=1, source_target_pairs={{0,3},{1,0},{2,1},{3,2},{4,7},{5,4},{6,5},{7,6},{8,11},{9,8},{10,9... | collective-permute-start | bytes 147848 | tf_op jit(solution)/shard_map/ppermute | solution.py:47
  33.0 1.9 %copy.62 = f32[128,32,128]{0,2,1:T(8,128)} copy(f32[128,32,128]{2,1,0:T(8,128)S(1)} %copy-done.5) | data formatting | bytes 4194304 | tf_op args[2]
  34.9 4.8 %fusion.26 = (f32[128,31,128]{0,2,1:T(8,128)}, f32[128,31,128]{0,2,1:T(8,128)}) fusion(f32[128,32,128]{0,2,1:T(8,128)} %copy.62), kind=kLoop, calls=%fused_computation.43 | loop fusion | bytes 8126464 | tf_op jit(solution)/shard_map/jit(_roll_static)/slice | solution.py:52
  39.7 0.9 fusion.27
  40.6 1.9 %copy.45 = f32[128,32,128]{0,2,1:T(8,128)} copy(f32[128,32,128]{2,1,0:T(8,128)S(1)} %copy-done) | data formatting | bytes 4194304 | tf_op args[0]
  42.5 0.0 collective-permute-done
  42.5 0.0 collective-permute-done.1
  42.5 1.8 %pad_maximum_fusion.3 = f32[128,32,130]{0,2,1:T(8,128)S(1)} fusion(f32[128,32,1]{0,2,1:T(1,128)S(1)} %bitcast.44, f32[128,32,128]{0,2,1:T(8,128)} %copy.45, f32[128,32,1]{0,2,1:T(1,128)S(1)} %bitcast.42), kind=kLoop, calls=%fused_computation.3 | loop fusion | flops 1064960 | bytes 4259840 | tf_op jit(solution)/shard_map/concatenate | solution.py:71
  44.3 0.3 fusion.24
  44.6 0.1 pad_maximum_fusion.10
  44.7 1.2 %copy-done.6 = f32[128,32,128]{0,2,1:T(8,128)S(1)} copy-done((f32[128,32,128]{0,2,1:T(8,128)S(1)}, f32[128,32,128]{0,2,1:T(8,128)}, u32[]{:S(2)}) %copy-start.6) | copy-done | bytes 2097176
  45.9 1.5 %fusion.6 = f32[128,32,130]{0,2,1:T(8,128)S(1)} fusion(f32[128,31,130]{0,2,1:T(8,128)S(1)} %get-tuple-element.10, f32[128,1,130]{0,2,1:T(8,128)S(1)} %get-tuple-element.12, f32[128,1,130]{0,2,1:T(8,128)S(1)} %get-tuple-element.11, f32[128,31,130]{0,2,1:T(8,128)S(1)} %get-tuple-element.9, f32[128,32,1]{0,2,1:T(1,128)S(1)} %bitcast.47, ...), kind=kLoop, calls=%fused_computation.9 | loop fusion | flops 7987200 | bytes 8569088 | tf_op jit(solution)/shard_map/add | solution.py:53
  47.4 0.0 copy-start.1
  47.5 0.5 fusion.22
  48.0 1.0 %copy-done.1 = f32[128,32,128]{0,2,1:T(8,128)S(1)} copy-done((f32[128,32,128]{0,2,1:T(8,128)S(1)}, f32[128,32,128]{0,2,1:T(8,128)}, u32[]{:S(2)}) %copy-start.1) | copy-done | bytes 2097176
  49.0 0.6 copy-done.7
  49.6 0.6 copy-done.8
  50.2 2.4 %fusion.14 = (f32[128,32,128]{0,2,1:T(8,128)S(1)}, f32[128,32,128]{0,2,1:T(8,128)S(1)}) fusion(f32[128,32,130]{0,2,1:T(8,128)S(1)} %fusion.6, f32[128,31,128]{0,2,1:T(8,128)S(1)} %get-tuple-element.6, f32[128,1,128]{0,2,1:T(8,128)S(1)} %get-tuple-element.8, f32[128,1,128]{0,2,1:T(8,128)S(1)} %get-tuple-element.7, f32[128,31,128]{0,2,1:T(8,128)S(1)} %get-tuple-element.5, ...), kind=kLoop, calls=%fused_computation.20 | loop fusion | flops 10485760 | bytes 21020672 | tf_op jit(solution)/shard_map/add | solution.py:53
  52.6 0.0 copy-start.4
  52.6 1.8 %fusion = f32[4,32,128]{2,0,1:T(4,128)S(1)} fusion(f32[4,256,1]{1,0,2:T(4,128)S(1)} %copy-done.12, f32[128,32,128]{0,2,1:T(8,128)S(1)} %get-tuple-element.30, f32[128,32,128]{0,2,1:T(8,128)S(1)} %get-tuple-element.29), kind=kOutput, calls=%fused_computation.1 | convolution fusion | flops 26214400 | bytes 4263936 | tf_op jit(solution)/shard_map/dot_general | solution.py:81
  54.5 0.2 copy-done.4
  54.6 0.0 collective-permute-start.2
  54.6 4.6 %collective-permute-done.2 = f32[4,32,128]{2,0,1:T(4,128)S(1)} collective-permute-done((f32[4,32,128]{2,0,1:T(4,128)S(1)}, f32[4,32,128]{2,0,1:T(4,128)S(1)}, u32[]{:S(2)}, u32[]{:S(2)}) %collective-permute-start.2) | collective-permute-done | bytes 65568 | tf_op jit(solution)/shard_map/ppermute | solution.py:92
  59.2 4.6 %collective-permute-done.3 = f32[4,32,128]{2,0,1:T(4,128)S(1)} collective-permute-done((f32[4,32,128]{2,0,1:T(4,128)S(1)}, f32[4,32,128]{2,0,1:T(4,128)S(1)}, u32[]{:S(2)}, u32[]{:S(2)}) %collective-permute-start.3) | collective-permute-done | bytes 65568 | tf_op jit(solution)/shard_map/ppermute | solution.py:92
  63.8 0.0 collective-permute-start.4
  63.8 4.6 %collective-permute-done.4 = f32[4,32,128]{2,0,1:T(4,128)S(1)} collective-permute-done((f32[4,32,128]{2,0,1:T(4,128)S(1)}, f32[4,32,128]{2,0,1:T(4,128)S(1)}, u32[]{:S(2)}, u32[]{:S(2)}) %collective-permute-start.4) | collective-permute-done | bytes 65568 | tf_op jit(solution)/shard_map/ppermute | solution.py:92
  68.4 4.6 %collective-permute-done.5 = f32[4,32,128]{2,0,1:T(4,128)S(1)} collective-permute-done((f32[4,32,128]{2,0,1:T(4,128)S(1)}, f32[4,32,128]{2,0,1:T(4,128)S(1)}, u32[]{:S(2)}, u32[]{:S(2)}) %collective-permute-start.5) | collective-permute-done | bytes 65568 | tf_op jit(solution)/shard_map/ppermute | solution.py:92
  73.0 4.6 %collective-permute-done.6 = f32[4,32,128]{2,0,1:T(4,128)S(1)} collective-permute-done((f32[4,32,128]{2,0,1:T(4,128)S(1)}, f32[4,32,128]{2,0,1:T(4,128)S(1)}, u32[]{:S(2)}, u32[]{:S(2)}) %collective-permute-start.6) | collective-permute-done | bytes 65568 | tf_op jit(solution)/shard_map/ppermute | solution.py:92
  77.6 0.0 collective-permute-start.7
  77.6 4.6 %collective-permute-done.7 = f32[4,32,128]{2,0,1:T(4,128)S(1)} collective-permute-done((f32[4,32,128]{2,0,1:T(4,128)S(1)}, f32[4,32,128]{2,0,1:T(4,128)S(1)}, u32[]{:S(2)}, u32[]{:S(2)}) %collective-permute-start.7) | collective-permute-done | bytes 65568 | tf_op jit(solution)/shard_map/ppermute | solution.py:92
  82.2 0.6 copy-done.9
  82.8 4.1 %collective-permute-done.8 = f32[4,32,128]{2,0,1:T(4,128)} collective-permute-done((f32[4,32,128]{2,0,1:T(4,128)S(1)}, f32[4,32,128]{2,0,1:T(4,128)}, u32[]{:S(2)}, u32[]{:S(2)}) %collective-permute-start.8) | collective-permute-done | bytes 65568 | tf_op jit(solution)/shard_map/ppermute | solution.py:92
  86.9 2.3 %concatenate.72 = f32[64,32,128]{2,0,1:T(8,128)S(1)} concatenate(f32[4,32,128]{2,0,1:T(4,128)} %collective-permute-done.8, f32[4,32,128]{2,0,1:T(4,128)} %copy-done.9, f32[4,32,128]{2,0,1:T(4,128)S(1)} %collective-permute-done.6, f32[4,32,128]{2,0,1:T(4,128)S(1)} %collective-permute-done.5, f32[4,32,128]{2,0,1:T(4,128)S(1)} %collective-permute-done.4, ...), dimensions={0} | concatenate | bytes 2097152 | tf_op jit(solution)/shard_map/jit(_roll_dynamic)/concatenate | solution.py:93
  89.1 0.0 copy-start.11
  89.2 1.1 %fusion.15 = f32[4,32,128]{2,0,1:T(4,128)S(1)} fusion(f32[64,32,128]{2,0,1:T(8,128)S(1)} %concatenate.72, s32[]{:T(128)S(6)} %select_n.19, f32[8,4,32]{2,1,0:T(4,128)} %constant.49.clone, s32[]{:T(128)S(6)} %select_n.17), kind=kOutput, calls=%fused_computation.25 | convolution fusion | flops 3145728 | bytes 591880 | tf_op jit(solution)/shard_map/dot_general | solution.py:81
  90.3 1.8 %fusion.32 = f32[32,128,128]{2,1,0:T(8,128)S(1)} fusion(f32[4,32,128]{2,0,1:T(4,128)S(1)} %fusion.15, f32[128,4,1]{0,1,2:T(4,128)S(1)} %copy-done.13), kind=kOutput, calls=%fused_computation.49 | convolution fusion | flops 12582912 | bytes 2164736 | tf_op jit(solution)/shard_map/dot_general | solution.py:81
  92.1 4.9 %bitcast_add_fusion = f32[128,32,128]{0,2,1:T(8,128)} fusion(f32[128,32,128]{0,2,1:T(8,128)S(1)} %copy-done.1, f32[32,128,128]{2,1,0:T(8,128)S(1)} %fusion.32, f32[128,256,1]{1,0,2:T(8,128)S(1)} %copy-done.11, f32[128,32,128]{0,2,1:T(8,128)} %copy-done.4, f32[128,32,128]{0,2,1:T(8,128)S(1)} %copy-done.3), kind=kOutput, calls=%fused_computation.24 | convolution fusion | flops 807403520 | bytes 10616832 | tf_op jit(solution)/shard_map/dot_general | solution.py:81
  97.0 3.0 %copy.65 = f32[128,32,128]{2,1,0:T(8,128)} copy(f32[128,32,128]{0,2,1:T(8,128)} %bitcast_add_fusion) | data formatting | bytes 4194304 | tf_op jit(solution)/shard_map/add | solution.py:100
  (31 shorter events, 0.1 us)
Async XLA Ops:
  8.7 5.5 %copy-start.5 = (f32[128,32,128]{2,1,0:T(8,128)S(1)}, f32[128,32,128]{2,1,0:T(8,128)}, u32[]{:S(2)}) copy-start(f32[128,32,128]{2,1,0:T(8,128)} %param.9) | copy-start | bytes 6291460
  17.0 2.7 %copy-start.10 = (f32[32,128]{1,0:T(8,128)S(1)}, f32[32,128]{1,0:T(8,128)}, u32[]{:S(2)}) copy-start(f32[32,128]{1,0:T(8,128)} %param.8) | copy-start | bytes 49156
  19.7 22.8 %collective-permute-start = (f32[385,32]{0,1:T(8,128)S(1)}, f32[385,32]{0,1:T(8,128)S(1)}, u32[]{:S(2)}, u32[]{:S(2)}) collective-permute-start(f32[385,32]{0,1:T(8,128)S(1)} %pad_maximum_fusion.8), channel_id=1, source_target_pairs={{0,1},{1,2},{2,3},{3,0},{4,5},{5,6},{6,7},{7,4},{8,9},{9,10},{10,1... | collective-permute-start | bytes 147848 | tf_op jit(solution)/shard_map/ppermute | solution.py:47
  30.8 11.7 %collective-permute-start.1 = (f32[385,32]{0,1:T(8,128)S(1)}, f32[385,32]{0,1:T(8,128)S(1)}, u32[]{:S(2)}, u32[]{:S(2)}) collective-permute-start(f32[385,32]{0,1:T(8,128)S(1)} %pad_maximum_fusion.9), channel_id=1, source_target_pairs={{0,3},{1,0},{2,1},{3,2},{4,7},{5,4},{6,5},{7,6},{8,11},{9,8},{10,9... | collective-permute-start | bytes 147848 | tf_op jit(solution)/shard_map/ppermute | solution.py:47
  34.9 5.7 %copy-start = (f32[128,32,128]{2,1,0:T(8,128)S(1)}, f32[128,32,128]{2,1,0:T(8,128)}, u32[]{:S(2)}) copy-start(f32[128,32,128]{2,1,0:T(8,128)} %param.7) | copy-start | bytes 6291460
  44.3 1.6 %copy-start.6 = (f32[128,32,128]{0,2,1:T(8,128)S(1)}, f32[128,32,128]{0,2,1:T(8,128)}, u32[]{:S(2)}) copy-start(f32[128,32,128]{0,2,1:T(8,128)} %copy.45) | copy-start | bytes 6291460
  47.4 1.6 %copy-start.1 = (f32[128,32,128]{0,2,1:T(8,128)S(1)}, f32[128,32,128]{0,2,1:T(8,128)}, u32[]{:S(2)}) copy-start(f32[128,32,128]{0,2,1:T(8,128)} %copy.62) | copy-start | bytes 6291460
  47.4 2.2 %copy-start.7 = (f32[128,31,128]{0,2,1:T(8,128)S(1)}, f32[128,31,128]{0,2,1:T(8,128)}, u32[]{:S(2)}) copy-start(f32[128,31,128]{0,2,1:T(8,128)} %get-tuple-element.13) | copy-start | bytes 6094852
  47.4 2.8 %copy-start.8 = (f32[128,31,128]{0,2,1:T(8,128)S(1)}, f32[128,31,128]{0,2,1:T(8,128)}, u32[]{:S(2)}) copy-start(f32[128,31,128]{0,2,1:T(8,128)} %get-tuple-element.14) | copy-start | bytes 6094852
  50.2 2.4 %copy-start.12 = (f32[4,256,1]{1,0,2:T(4,128)S(1)}, f32[4,256,1]{1,0,2:T(4,128)}, u32[]{:S(2)}) copy-start(f32[4,256,1]{1,0,2:T(4,128)} %constant.53) | copy-start | bytes 12292
  52.6 1.8 %copy-start.2 = (f32[128,32,128]{0,2,1:T(8,128)}, f32[128,32,128]{0,2,1:T(8,128)S(1)}, u32[]{:S(2)}) copy-start(f32[128,32,128]{0,2,1:T(8,128)S(1)} %get-tuple-element.29) | copy-start | bytes 6291460
  52.6 2.0 %copy-start.4 = (f32[128,32,128]{0,2,1:T(8,128)}, f32[128,32,128]{0,2,1:T(8,128)S(1)}, u32[]{:S(2)}) copy-start(f32[128,32,128]{0,2,1:T(8,128)S(1)} %get-tuple-element.30) | copy-start | bytes 6291460
  54.6 35.6 %copy-start.13 = (f32[128,4,1]{0,1,2:T(4,128)S(1)}, f32[128,4,1]{0,1,2:T(4,128)}, u32[]{:S(2)}) copy-start(f32[128,4,1]{0,1,2:T(4,128)} %constant.54) | copy-start | bytes 6148
  54.6 4.6 %collective-permute-start.2 = (f32[4,32,128]{2,0,1:T(4,128)S(1)}, f32[4,32,128]{2,0,1:T(4,128)S(1)}, u32[]{:S(2)}, u32[]{:S(2)}) collective-permute-start(f32[4,32,128]{2,0,1:T(4,128)S(1)} %fusion), channel_id=1, source_target_pairs={{0,4},{4,8},{8,12},{12,16},{16,20},{20,24},{24,28},{28,0},{1,5},{5... | collective-permute-start | bytes 196616 | tf_op jit(solution)/shard_map/ppermute | solution.py:92
  59.2 4.6 %collective-permute-start.3 = (f32[4,32,128]{2,0,1:T(4,128)S(1)}, f32[4,32,128]{2,0,1:T(4,128)S(1)}, u32[]{:S(2)}, u32[]{:S(2)}) collective-permute-start(f32[4,32,128]{2,0,1:T(4,128)S(1)} %collective-permute-done.2), channel_id=1, source_target_pairs={{0,4},{4,8},{8,12},{12,16},{16,20},{20,24},{24,28},{28,0},{1,5},{5... | collective-permute-start | bytes 196616 | tf_op jit(solution)/shard_map/ppermute | solution.py:92
  63.8 4.6 %collective-permute-start.4 = (f32[4,32,128]{2,0,1:T(4,128)S(1)}, f32[4,32,128]{2,0,1:T(4,128)S(1)}, u32[]{:S(2)}, u32[]{:S(2)}) collective-permute-start(f32[4,32,128]{2,0,1:T(4,128)S(1)} %collective-permute-done.3), channel_id=1, source_target_pairs={{0,4},{4,8},{8,12},{12,16},{16,20},{20,24},{24,28},{28,0},{1,5},{5... | collective-permute-start | bytes 196616 | tf_op jit(solution)/shard_map/ppermute | solution.py:92
  68.4 4.6 %collective-permute-start.5 = (f32[4,32,128]{2,0,1:T(4,128)S(1)}, f32[4,32,128]{2,0,1:T(4,128)S(1)}, u32[]{:S(2)}, u32[]{:S(2)}) collective-permute-start(f32[4,32,128]{2,0,1:T(4,128)S(1)} %collective-permute-done.4), channel_id=1, source_target_pairs={{0,4},{4,8},{8,12},{12,16},{16,20},{20,24},{24,28},{28,0},{1,5},{5... | collective-permute-start | bytes 196616 | tf_op jit(solution)/shard_map/ppermute | solution.py:92
  73.0 4.6 %collective-permute-start.6 = (f32[4,32,128]{2,0,1:T(4,128)S(1)}, f32[4,32,128]{2,0,1:T(4,128)S(1)}, u32[]{:S(2)}, u32[]{:S(2)}) collective-permute-start(f32[4,32,128]{2,0,1:T(4,128)S(1)} %collective-permute-done.5), channel_id=1, source_target_pairs={{0,4},{4,8},{8,12},{12,16},{16,20},{20,24},{24,28},{28,0},{1,5},{5... | collective-permute-start | bytes 196616 | tf_op jit(solution)/shard_map/ppermute | solution.py:92
  77.6 4.6 %collective-permute-start.7 = (f32[4,32,128]{2,0,1:T(4,128)S(1)}, f32[4,32,128]{2,0,1:T(4,128)S(1)}, u32[]{:S(2)}, u32[]{:S(2)}) collective-permute-start(f32[4,32,128]{2,0,1:T(4,128)S(1)} %collective-permute-done.6), channel_id=1, source_target_pairs={{0,4},{4,8},{8,12},{12,16},{16,20},{20,24},{24,28},{28,0},{1,5},{5... | collective-permute-start | bytes 196616 | tf_op jit(solution)/shard_map/ppermute | solution.py:92
  82.2 0.6 copy-start.9
  82.2 4.7 %collective-permute-start.8 = (f32[4,32,128]{2,0,1:T(4,128)S(1)}, f32[4,32,128]{2,0,1:T(4,128)}, u32[]{:S(2)}, u32[]{:S(2)}) collective-permute-start(f32[4,32,128]{2,0,1:T(4,128)S(1)} %collective-permute-done.7), channel_id=1, source_target_pairs={{0,4},{4,8},{8,12},{12,16},{16,20},{20,24},{24,28},{28,0},{1,5},{5... | collective-permute-start | bytes 196616 | tf_op jit(solution)/shard_map/ppermute | solution.py:92
  89.1 3.0 %copy-start.3 = (f32[128,32,128]{0,2,1:T(8,128)S(1)}, f32[128,32,128]{0,2,1:T(8,128)}, u32[]{:S(2)}) copy-start(f32[128,32,128]{0,2,1:T(8,128)} %copy-done.2) | copy-start | bytes 6291460
  89.1 3.0 %copy-start.11 = (f32[128,256,1]{1,0,2:T(8,128)S(1)}, f32[128,256,1]{1,0,2:T(8,128)}, u32[]{:S(2)}) copy-start(f32[128,256,1]{1,0,2:T(8,128)} %constant.52) | copy-start | bytes 393220
